TPU v7x, 256 devices: a whole 4x4x8 slice. The times are simulated.
256 devices in a mesh: rep: 32 (over y, x, core), tp: 8 (over z).
Axes of the slice: x: 4, y: 4, z: 8, core: 2. Of those that a mesh axis runs over, the one named last changes fastest.
Arguments:
- queries: bfloat16 [8192, 4096], P('rep', 'tp'), may hold values from -120 to 120
- keys_new: bfloat16 [8192, 1024], P('rep', 'tp'), may hold values from -7 to 7
- values_new: bfloat16 [8192, 1024], P('rep', 'tp'), may hold values from -6 to 6
- caches: bfloat16 [64, 2, 4096, 1024], P('rep', None, None, 'tp'), may hold values from -6 to 6
- lengths: int32 [32, 2], replicated, may hold values from 128 to 4096, as said below
- moving: int32 [32], replicated, may hold values from 0 to 1
- destination: int32 [32], replicated, may hold values from 0 to 31, each once
- out_weight: bfloat16 [4096, 4096], P('tp'), may hold values from -0.09375 to 0.09375
Outputs:
- mixed: bfloat16 [8192, 4096], P('rep', 'tp')
- held_cache: bfloat16 [64, 2, 4096, 1024], P('rep', None, None, 'tp')
Inputs may be any that keep to these rules, and one draw needn't show every extreme that they name: `lengths`: multiples of 128; in every draw some slot holds 4096 and some 128. `destination`: each replica receives exactly one failing candidate; it takes the slot that its own failing candidate leaves.
All inputs are finite; a program needn't handle non-finite values.
Results may differ from a plain program's by a relative error of at most 0.014.
Values may be sent and summed in bfloat16 or wider, within the bound.
No kernel may reach another device: no remote copies, remote signals or barrier semaphores. Data moves between devices by JAX's collectives and lax.ppermute only.
A program may use at most 64 MiB of HBM per device.

v0:
```python
import functools

import jax
import jax.numpy as jnp
from jax import lax
from jax.experimental import pallas as pl
from jax.experimental.pallas import tpu as pltpu
from jax.sharding import Mesh
from jax.sharding import PartitionSpec as P

HEAD = 128
REP = ("rep_0", "rep_1", "rep_2")
LOG2E = 1.4426950408889634
MASKED = -1e30
CHUNK = 2048
PARTS = (1, 1, 1, 1, 2, 1, 1, 1)


def place():
    return lax.axis_index(REP).astype(jnp.int32), lax.axis_index("tp").astype(jnp.int32)


def pick_kernel(moving, caches, sent, held, in_sems, out_sems):
    own, _ = place()
    leaving = moving[own]
    pieces = in_sems.shape[0]
    rows = sent.shape[0] // pieces

    def load(i):
        piece = pl.ds(i * rows, rows)
        return pltpu.make_async_copy(caches.at[leaving, piece], held.at[piece], in_sems.at[i])

    def save(i):
        piece = pl.ds(i * rows, rows)
        return pltpu.make_async_copy(held.at[piece], sent.at[piece], out_sems.at[i])

    for i in range(pieces):
        load(i).start()
    for i in range(pieces):
        load(i).wait()
        save(i).start()
    for i in range(pieces):
        save(i).wait()


def pick(moving, caches):
    slots, _, rows, _ = caches.shape
    hbm = pl.BlockSpec(memory_space=pltpu.HBM)
    caches = pltpu.with_memory_space_constraint(caches.reshape(slots, 2 * rows, HEAD), pltpu.HBM)
    return pl.pallas_call(
        pick_kernel,
        out_shape=jax.ShapeDtypeStruct((2 * rows, HEAD), caches.dtype),
        in_specs=[pl.BlockSpec(memory_space=pltpu.SMEM), hbm],
        out_specs=hbm,
        scratch_shapes=[
            pltpu.VMEM((2 * rows, HEAD), caches.dtype),
            pltpu.SemaphoreType.DMA((8,)),
            pltpu.SemaphoreType.DMA((8,)),
        ],
        compiler_params=pltpu.CompilerParams(vmem_limit_bytes=60 * 2**20),
        cost_estimate=pl.CostEstimate(flops=0, bytes_accessed=8 * rows * HEAD, transcendentals=0),
        name="pick",
    )(moving, caches)


def slot_kernel(arrived, group, chunk, parts, lengths, moving, destination, queries, keys_new, values_new, cache, weight, *rest):
    scratch = 10
    if arrived:
        rest = rest[1:]
    held = rest[0]
    outs = rest[1:-scratch]
    (kbuf, vbuf, wbuf, top_ref, sum_ref, acc, obuf, in_sem, out_sem, sems) = rest[-scratch:]
    own, me = place()
    replicas = destination.shape[0]
    chunks = cache.shape[2] // chunk
    span = obuf.shape[0]
    peers = len(parts)
    leaving = moving[own]
    if arrived:
        source, target = 0, leaving
        anchor = jnp.int32(0)
        for r in range(replicas):
            anchor = jnp.where(destination[r] == own, r, anchor)
        length = lengths[anchor, moving[anchor]]
    else:
        source = target = 1 - leaving
        length = lengths[own, target]

    def load(c):
        piece = pl.ds(c * chunk, chunk)
        return (
            pltpu.make_async_copy(cache.at[source, 0, piece], kbuf.at[piece], in_sem.at[0, c]),
            pltpu.make_async_copy(cache.at[source, 1, piece], vbuf.at[piece], in_sem.at[1, c]),
        )

    def save(c):
        piece = pl.ds(c * chunk, chunk)
        return (
            pltpu.make_async_copy(kept(0, piece), held.at[target, 0, piece], out_sem.at[0, c]),
            pltpu.make_async_copy(kept(1, piece), held.at[target, 1, piece], out_sem.at[1, c]),
        )

    def kept(which, piece):
        if arrived:
            return cache.at[0, which, piece]
        return (kbuf, vbuf)[which].at[piece]

    own_rows = pl.ds(pl.multiple_of(target * span, span), span)
    weight_copy = pltpu.make_async_copy(weight, wbuf, sems.at[3])
    for c in range(chunks):
        for copy in save(c) if arrived else load(c):
            copy.start()
    weight_copy.start()

    factor = HEAD**-0.5 * LOG2E
    rows = group * span
    over_head = (((1,), (1,)), ((), ()))
    over_keys = (((0,), (0,)), ((), ()))
    grouped = jnp.concatenate([queries[own_rows, pl.ds(h * HEAD, HEAD)] for h in range(group)], axis=0)
    key_at = lax.broadcasted_iota(jnp.int32, (span, rows), 0)
    row_at = lax.rem(lax.broadcasted_iota(jnp.int32, (span, rows), 1), span)
    scores = lax.dot_general(keys_new[own_rows, :], grouped, over_head, preferred_element_type=jnp.float32)
    scores = jnp.where(key_at <= row_at, scores * factor, MASKED)
    top = jnp.max(scores, axis=0, keepdims=True)
    weights = jnp.exp2(scores - top)
    top_ref[...] = top
    sum_ref[...] = jnp.sum(weights, axis=0, keepdims=True)
    acc[...] = lax.dot_general(
        values_new[own_rows, :], weights.astype(jnp.bfloat16), over_keys, preferred_element_type=jnp.float32
    )

    def step(c, _):
        if not arrived:
            for copy in load(c):
                copy.wait()
            for copy in save(c):
                copy.start()

        @pl.when(c * chunk < length)
        def _():
            piece = pl.ds(pl.multiple_of(c * chunk, chunk), chunk)
            scores = lax.dot_general(kept(0, piece)[...], grouped, over_head, preferred_element_type=jnp.float32)
            seen = lax.broadcasted_iota(jnp.int32, (chunk, rows), 0) < length - c * chunk
            scores = jnp.where(seen, scores * factor, MASKED)
            before = top_ref[...]
            top = jnp.maximum(before, jnp.max(scores, axis=0, keepdims=True))
            shrink = jnp.exp2(before - top)
            weights = jnp.exp2(scores - top)
            top_ref[...] = top
            sum_ref[...] = sum_ref[...] * shrink + jnp.sum(weights, axis=0, keepdims=True)
            acc[...] = acc[...] * shrink + lax.dot_general(
                kept(1, piece)[...], weights.astype(jnp.bfloat16), over_keys, preferred_element_type=jnp.float32
            )

        return 0

    lax.fori_loop(0, chunks, step, 0)
    result = acc[...] / sum_ref[...]
    for h in range(group):
        obuf[:, pl.ds(h * HEAD, HEAD)] = result[:, h * span : (h + 1) * span].T.astype(jnp.bfloat16)
    weight_copy.wait()
    width = wbuf.shape[1] // peers
    out = 0
    for k in range(peers):
        columns = pl.ds(pl.multiple_of(lax.rem(me + k, peers) * width, width), width)
        block = jnp.dot(obuf[...], wbuf[:, columns], preferred_element_type=jnp.float32)
        block = block.astype(jnp.bfloat16)
        height = span // parts[k]
        for part in range(parts[k]):
            outs[out][...] = block[part * height : (part + 1) * height]
            out += 1
    for c in range(chunks):
        for copy in save(c):
            copy.wait()


def run_slot(lengths, moving, destination, queries, keys_new, values_new, cache, weight, parts, held=None):
    span = queries.shape[0] // lengths.shape[1]
    slots = lengths.shape[1]
    group = queries.shape[1] // HEAD
    rows = cache.shape[2]
    peers = len(parts)
    chunks = rows // CHUNK
    kept = rows if held is None else 16
    width = weight.shape[1] // peers
    smem = pl.BlockSpec(memory_space=pltpu.SMEM)
    vmem = pl.BlockSpec(memory_space=pltpu.VMEM)
    hbm = pl.BlockSpec(memory_space=pltpu.HBM)
    weight = pltpu.with_memory_space_constraint(weight, pltpu.HBM)
    if held is None:
        cache = pltpu.with_memory_space_constraint(cache, pltpu.HBM)
    operands = [lengths, moving, destination, queries, keys_new, values_new, cache, weight]
    in_specs = [smem] * 3 + [vmem] * 3
    in_specs += [hbm if held is None else vmem, hbm]
    aliases = {}
    if held is not None:
        operands.append(held)
        in_specs.append(hbm)
        aliases = {8: 0}
    shapes = [jax.ShapeDtypeStruct((slots, 2, rows, HEAD), cache.dtype)]
    for count in parts:
        shapes += [jax.ShapeDtypeStruct((span // count, width), jnp.bfloat16)] * count
    flops = 4 * group * span * HEAD * (rows + span) + 2 * span * weight.shape[0] * weight.shape[1]
    return pl.pallas_call(
        functools.partial(slot_kernel, held is not None, group, CHUNK, parts),
        out_shape=shapes,
        in_specs=in_specs,
        out_specs=[hbm] + [vmem] * (len(shapes) - 1),
        scratch_shapes=[
            pltpu.VMEM((kept, HEAD), jnp.bfloat16),
            pltpu.VMEM((kept, HEAD), jnp.bfloat16),
            pltpu.VMEM(weight.shape, jnp.bfloat16),
            pltpu.VMEM((1, group * span), jnp.float32),
            pltpu.VMEM((1, group * span), jnp.float32),
            pltpu.VMEM((HEAD, group * span), jnp.float32),
            pltpu.VMEM((span, group * HEAD), jnp.bfloat16),
            pltpu.SemaphoreType.DMA((2, chunks)),
            pltpu.SemaphoreType.DMA((2, chunks)),
            pltpu.SemaphoreType.DMA((4,)),
        ],
        input_output_aliases=aliases,
        compiler_params=pltpu.CompilerParams(vmem_limit_bytes=32 * 2**20),
        cost_estimate=pl.CostEstimate(
            flops=flops,
            bytes_accessed=8 * rows * HEAD + weight.size * 2,
            transcendentals=group * span * rows,
        ),
        name="slot",
    )(*operands)


def shift(block, k):
    peers = lax.axis_size("tp")
    return lax.ppermute(block, "tp", [(i, (i + k) % peers) for i in range(peers)])


def widen(block):
    return block.astype(jnp.float32)


def far_sums(blocks):
    b0, b1, b2, b3, b4_low, b4_high, b5, b6, b7 = blocks
    right = shift(b3, 1)
    left = shift(b5, -1)
    low = shift(b4_low, 2)
    high = shift(b4_high, -2)
    one = shift(b1, 1)
    seven = shift(b7, -1)
    none = jnp.zeros_like(low)
    right = widen(b2) + widen(right) + widen(jnp.concatenate([low, none]))
    left = widen(b6) + widen(left) + widen(jnp.concatenate([none, high]))
    return b0, one, seven, right.astype(jnp.bfloat16), left.astype(jnp.bfloat16)


def owner_sum(b0, one, seven, right, left):
    two = shift(right, 2)
    six = shift(left, -2)
    return widen(b0) + widen(one) + widen(seven) + widen(two) + widen(six)


def on_device(queries, keys_new, values_new, caches, lengths, moving, destination, out_weight):
    replicas = lax.axis_size(REP)
    slots, _, rows, _ = caches.shape
    span = queries.shape[0] // slots
    order = jnp.arange(replicas, dtype=jnp.int32)
    source_of = jnp.sum(jnp.where(destination[None, :] == order[:, None], order[None, :], 0), axis=1)
    small = (lengths, moving, destination, queries, keys_new, values_new)

    sent = pick(moving, caches).reshape(replicas, 2 * rows // replicas, HEAD)
    spread = lax.all_to_all(sent, REP, 0, 0, tiled=True)
    held, *stay = run_slot(*small, caches, out_weight, PARTS)
    stay = far_sums(stay)
    spread, stay = lax.optimization_barrier((spread, stay))
    ordered = spread.at[source_of].get(mode="promise_in_bounds")
    arrived = lax.all_to_all(ordered, REP, 0, 0, tiled=True)
    stay_mixed = owner_sum(*stay).astype(jnp.bfloat16)

    leaving = moving[lax.axis_index(REP)]
    own = lax.broadcasted_iota(jnp.int32, (slots, 1, 1), 0) == leaving
    arrived, stay_mixed, own = lax.optimization_barrier((arrived, stay_mixed, own))
    arrived = arrived.reshape(1, 2, rows, HEAD)
    held, *move = run_slot(*small, arrived, out_weight, PARTS, held)
    move_mixed = owner_sum(*far_sums(move)).astype(jnp.bfloat16)
    mixed = jnp.where(own, move_mixed[None], stay_mixed[None])
    return mixed.reshape(slots * span, -1), held


def solution(mesh):
    split = Mesh(mesh.devices.reshape(4, 4, 2, mesh.shape["tp"]), REP + ("tp",))
    return jax.shard_map(
        on_device,
        mesh=split,
        in_specs=(
            P(REP, "tp"),
            P(REP, "tp"),
            P(REP, "tp"),
            P(REP, None, None, "tp"),
            P(),
            P(),
            P(),
            P("tp", None),
        ),
        out_specs=(P(REP, "tp"), P(REP, None, None, "tp")),
        check_vma=False,
    )
```

profile of v0, /device:TPU:64, one launch (start us, length us, event | category | flops | bytes accessed | tf_op | source)
XLA Modules:
  0.0 109.0 jit_solution(9373959203192320712)
XLA Ops:
  0.6 3.1 %pick.1 = bf16[8192,128]{1,0:T(8,128)(2,1)} custom-call(s32[32]{0:T(128)} %moving.5, bf16[2,8192,128]{2,1,0:T(8,128)(2,1)} %bitcast.16), custom_call_target="tpu_custom_call" | custom-call | bytes 4194304 | tf_op jit(solution)/shard_map/pick/pallas_call | solution.py:50
  3.8 7.5 %all-to-all-start = ((bf16[32,256,128]{2,1,0:T(8,128)(2,1)}), bf16[32,256,128]{2,1,0:T(8,128)(2,1)S(1)}, u32[]{:S(2)}, u32[]{:S(2)}) async-start(bf16[32,256,128]{2,1,0:T(8,128)(2,1)} %bitcast.17), calls=%async_computation | async-start | bytes 4194304 | tf_op jit(solution)/shard_map/all_to_all | solution.py:270
  11.3 0.1 copy.13.lengths
  11.4 5.0 %slot.2 = (bf16[2,2,4096,128]{3,2,1,0:T(8,128)(2,1)}, bf16[128,512]{1,0:T(8,128)(2,1)S(1)}, bf16[128,512]{1,0:T(8,128)(2,1)S(1)}, bf16[128,512]{1,0:T(8,128)(2,1...) custom-call(s32[32,2]{1,0:T(8,128)S(1)} %copy.13.lengths, ...), custom_call_target="tpu_custom_call" | custom-call | flops 1644167168 | bytes 8388608 | tf_op jit(solution)/shard_map/slot/pallas_call | solution.py:204
  16.4 4.5 %collective-permute-start.3 = (bf16[64,512]{1,0:T(8,128)(2,1)S(1)}, bf16[64,512]{1,0:T(8,128)(2,1)S(1)}, u32[]{:S(2)}, u32[]{:S(2)}) collective-permute-start(bf16[64,512]{1,0:T(8,128)(2,1)S(1)} %get-tuple-element.36), channel_id=1, source_target_pairs={{0,2},{1,3},{2,4},{3,5},{4,6},{5,7},{6,0},{7,1},{8,10},{9,11},{10,... | collective-permute-start | bytes 196616 | tf_op jit(solution)/shard_map/ppermute | solution.py:234
  20.9 1.0 collective-permute-start
  22.0 1.0 collective-permute-start.1
  23.0 2.7 %collective-permute-start.2 = (bf16[128,512]{1,0:T(8,128)(2,1)S(1)}, bf16[128,512]{1,0:T(8,128)(2,1)S(1)}, u32[]{:S(2)}, u32[]{:S(2)}) collective-permute-start(bf16[128,512]{1,0:T(8,128)(2,1)S(1)} %get-tuple-element.35), channel_id=1, source_target_pairs={{0,1},{1,2},{2,3},{3,4},{4,5},{5,6},{6,7},{7,0},{8,9},{9,10},{10,1... | collective-permute-start | bytes 393224 | tf_op jit(solution)/shard_map/ppermute | solution.py:234
  25.6 0.1 select_reduce_fusion
  25.9 3.7 %collective-permute-done.2 = bf16[128,512]{1,0:T(8,128)(2,1)S(1)} collective-permute-done((bf16[128,512]{1,0:T(8,128)(2,1)S(1)}, bf16[128,512]{1,0:T(8,128)(2,1)S(1)}, u32[]{:S(2)}, u32[]{:S(2)}) %collective-permute-start.2) | collective-permute-done | bytes 131104 | tf_op jit(solution)/shard_map/ppermute | solution.py:234
  29.6 3.9 %collective-permute-done.4 = bf16[128,512]{1,0:T(8,128)(2,1)S(1)} collective-permute-done((bf16[128,512]{1,0:T(8,128)(2,1)S(1)}, bf16[128,512]{1,0:T(8,128)(2,1)S(1)}, u32[]{:S(2)}, u32[]{:S(2)}) %collective-permute-start.4) | collective-permute-done | bytes 131104 | tf_op jit(solution)/shard_map/ppermute | solution.py:234
  33.5 7.8 %all-to-all-done = bf16[32,256,128]{2,1,0:T(8,128)(2,1)S(1)} async-done(((bf16[32,256,128]{2,1,0:T(8,128)(2,1)}), bf16[32,256,128]{2,1,0:T(8,128)(2,1)S(1)}, u32[]{:S(2)}, u32[]{:S(2)}) %all-to-all-start) | async-done | bytes 2097184 | tf_op jit(solution)/shard_map/all_to_all | solution.py:270
  41.4 2.1 %gather_fusion = bf16[32,256,128]{2,1,0:T(8,128)(2,1)} fusion(bf16[32,256,128]{2,1,0:T(8,128)(2,1)S(1)} %all-to-all-done, s32[1024]{0:T(1024)S(1)} %pad_clamp_fusion), kind=kCustom, calls=%fused_computation | custom fusion | bytes 4194432 | tf_op jit(solution)/shard_map/gather | solution.py:274
  43.5 4.0 %all-to-all-start.1 = ((bf16[32,256,128]{2,1,0:T(8,128)(2,1)}), bf16[32,256,128]{2,1,0:T(8,128)(2,1)S(1)}, u32[]{:S(2)}, u32[]{:S(2)}) async-start(bf16[32,256,128]{2,1,0:T(8,128)(2,1)} %gather_fusion), calls=%async_computation.1 | async-start | bytes 4194304 | tf_op jit(solution)/shard_map/all_to_all | solution.py:275
  47.5 4.6 %collective-permute-start.6 = (bf16[128,512]{1,0:T(8,128)(2,1)S(1)}, bf16[128,512]{1,0:T(8,128)(2,1)S(1)}, u32[]{:S(2)}, u32[]{:S(2)}) collective-permute-start(bf16[128,512]{1,0:T(8,128)(2,1)S(1)} %add_convert_fusion.5), channel_id=1, source_target_pairs={{0,2},{1,3},{2,4},{3,5},{4,6},{5,7},{6,0},{7,1},{8,10},{9,11},{10,... | collective-permute-start | bytes 393224 | tf_op jit(solution)/shard_map/ppermute | solution.py:234
  52.1 0.6 dynamic_slice.3
  52.7 0.7 iota_compare_fusion.1
  53.3 4.5 %collective-permute-done.6 = bf16[128,512]{1,0:T(8,128)(2,1)S(1)} collective-permute-done((bf16[128,512]{1,0:T(8,128)(2,1)S(1)}, bf16[128,512]{1,0:T(8,128)(2,1)S(1)}, u32[]{:S(2)}, u32[]{:S(2)}) %collective-permute-start.6) | collective-permute-done | bytes 131104 | tf_op jit(solution)/shard_map/ppermute | solution.py:234
  57.9 4.3 %collective-permute-done.7 = bf16[128,512]{1,0:T(8,128)(2,1)S(1)} collective-permute-done((bf16[128,512]{1,0:T(8,128)(2,1)S(1)}, bf16[128,512]{1,0:T(8,128)(2,1)S(1)}, u32[]{:S(2)}, u32[]{:S(2)}) %collective-permute-start.7) | collective-permute-done | bytes 131104 | tf_op jit(solution)/shard_map/ppermute | solution.py:234
  62.3 15.3 %all-to-all-done.1 = bf16[32,256,128]{2,1,0:T(8,128)(2,1)S(1)} async-done(((bf16[32,256,128]{2,1,0:T(8,128)(2,1)}), bf16[32,256,128]{2,1,0:T(8,128)(2,1)S(1)}, u32[]{:S(2)}, u32[]{:S(2)}) %all-to-all-start.1) | async-done | bytes 2097184 | tf_op jit(solution)/shard_map/all_to_all | solution.py:275
  77.6 5.9 %slot.3 = (bf16[2,2,4096,128]{3,2,1,0:T(8,128)(2,1)}, bf16[128,512]{1,0:T(8,128)(2,1)S(1)}, bf16[128,512]{1,0:T(8,128)(2,1)S(1)}, bf16[128,512]{1,0:T(8,128)(2,1...) custom-call(s32[32,2]{1,0:T(8,128)S(1)} %copy.13.lengths, ...), custom_call_target="tpu_custom_call", output_to_operand_aliasing={{0}: (8, {})} | custom-call | flops 1644167168 | bytes 8388608 | tf_op jit(solution)/shard_map/slot/pallas_call | solution.py:204
  83.5 2.0 %collective-permute-start.10 = (bf16[128,512]{1,0:T(8,128)(2,1)S(1)}, bf16[128,512]{1,0:T(8,128)(2,1)S(1)}, u32[]{:S(2)}, u32[]{:S(2)}) collective-permute-start(bf16[128,512]{1,0:T(8,128)(2,1)S(1)} %get-tuple-element.53), channel_id=1, source_target_pairs={{0,1},{1,2},{2,3},{3,4},{4,5},{5,6},{6,7},{7,0},{8,9},{9,10},{10,1... | collective-permute-start | bytes 393224 | tf_op jit(solution)/shard_map/ppermute | solution.py:234
  85.5 3.6 %collective-permute-start.11 = (bf16[64,512]{1,0:T(8,128)(2,1)S(1)}, bf16[64,512]{1,0:T(8,128)(2,1)S(1)}, u32[]{:S(2)}, u32[]{:S(2)}) collective-permute-start(bf16[64,512]{1,0:T(8,128)(2,1)S(1)} %get-tuple-element.54), channel_id=1, source_target_pairs={{0,2},{1,3},{2,4},{3,5},{4,6},{5,7},{6,0},{7,1},{8,10},{9,11},{10,... | collective-permute-start | bytes 196616 | tf_op jit(solution)/shard_map/ppermute | solution.py:234
  89.1 2.4 %collective-permute-start.8 = (bf16[128,512]{1,0:T(8,128)(2,1)S(1)}, bf16[128,512]{1,0:T(8,128)(2,1)S(1)}, u32[]{:S(2)}, u32[]{:S(2)}) collective-permute-start(bf16[128,512]{1,0:T(8,128)(2,1)S(1)} %get-tuple-element.50), channel_id=1, source_target_pairs={{0,1},{1,2},{2,3},{3,4},{4,5},{5,6},{6,7},{7,0},{8,9},{9,10},{10,1... | collective-permute-start | bytes 393224 | tf_op jit(solution)/shard_map/ppermute | solution.py:234
  91.5 0.7 collective-permute-done.11
  92.2 2.5 %collective-permute-start.13 = (bf16[128,512]{1,0:T(8,128)(2,1)S(1)}, bf16[128,512]{1,0:T(8,128)(2,1)S(1)}, u32[]{:S(2)}, u32[]{:S(2)}) collective-permute-start(bf16[128,512]{1,0:T(8,128)(2,1)S(1)} %get-tuple-element.56), channel_id=1, source_target_pairs={{0,7},{1,0},{2,1},{3,2},{4,3},{5,4},{6,5},{7,6},{8,15},{9,8},{10,9... | collective-permute-start | bytes 393224 | tf_op jit(solution)/shard_map/ppermute | solution.py:234
  94.7 2.3 %collective-permute-start.12 = (bf16[128,512]{1,0:T(8,128)(2,1)S(1)}, bf16[128,512]{1,0:T(8,128)(2,1)S(1)}, u32[]{:S(2)}, u32[]{:S(2)}) collective-permute-start(bf16[128,512]{1,0:T(8,128)(2,1)S(1)} %add_convert_fusion.2), channel_id=1, source_target_pairs={{0,2},{1,3},{2,4},{3,5},{4,6},{5,7},{6,0},{7,1},{8,10},{9,11},{10,... | collective-permute-start | bytes 393224 | tf_op jit(solution)/shard_map/ppermute | solution.py:234
  97.1 2.2 %collective-permute-done.13 = bf16[128,512]{1,0:T(8,128)(2,1)S(1)} collective-permute-done((bf16[128,512]{1,0:T(8,128)(2,1)S(1)}, bf16[128,512]{1,0:T(8,128)(2,1)S(1)}, u32[]{:S(2)}, u32[]{:S(2)}) %collective-permute-start.13) | collective-permute-done | bytes 131104 | tf_op jit(solution)/shard_map/ppermute | solution.py:234
  99.3 2.1 %collective-permute-start.15 = (bf16[128,512]{1,0:T(8,128)(2,1)S(1)}, bf16[128,512]{1,0:T(8,128)(2,1)S(1)}, u32[]{:S(2)}, u32[]{:S(2)}) collective-permute-start(bf16[128,512]{1,0:T(8,128)(2,1)S(1)} %add_convert_fusion.1), channel_id=1, source_target_pairs={{0,6},{1,7},{2,0},{3,1},{4,2},{5,3},{6,4},{7,5},{8,14},{9,15},{10,... | collective-permute-start | bytes 393224 | tf_op jit(solution)/shard_map/ppermute | solution.py:234
  101.6 6.6 %collective-permute-done.15 = bf16[128,512]{1,0:T(8,128)(2,1)S(1)} collective-permute-done((bf16[128,512]{1,0:T(8,128)(2,1)S(1)}, bf16[128,512]{1,0:T(8,128)(2,1)S(1)}, u32[]{:S(2)}, u32[]{:S(2)}) %collective-permute-start.15) | collective-permute-done | bytes 131104 | tf_op jit(solution)/shard_map/ppermute | solution.py:234
  108.1 0.1 add_convert_fusion
  108.2 0.8 bitcast_select_fusion
  (34 shorter events, 0.5 us)
Async XLA Ops:
  3.7 7.5 %copy-start.5 = (s32[32,2]{0,1:T(2,128)S(1)}, s32[32,2]{0,1:T(2,128)}, u32[]{:S(2)}) copy-start(s32[32,2]{0,1:T(2,128)} %param.12) | copy-start | bytes 772
  3.8 7.6 %copy-start = (bf16[256,512]{1,0:T(8,128)(2,1)S(1)}, bf16[256,512]{1,0:T(8,128)(2,1)}, u32[]{:S(2)}) copy-start(bf16[256,512]{1,0:T(8,128)(2,1)} %queries.3) | copy-start | bytes 786436
  3.8 7.6 %copy-start.1 = (bf16[256,128]{1,0:T(8,128)(2,1)S(1)}, bf16[256,128]{1,0:T(8,128)(2,1)}, u32[]{:S(2)}) copy-start(bf16[256,128]{1,0:T(8,128)(2,1)} %keys_new.3) | copy-start | bytes 196612
  3.8 7.6 %copy-start.2 = (bf16[256,128]{1,0:T(8,128)(2,1)S(1)}, bf16[256,128]{1,0:T(8,128)(2,1)}, u32[]{:S(2)}) copy-start(bf16[256,128]{1,0:T(8,128)(2,1)} %values_new.3) | copy-start | bytes 196612
  3.8 7.6 %copy-start.3 = (s32[32]{0:T(128)S(1)}, s32[32]{0:T(128)}, u32[]{:S(2)}) copy-start(s32[32]{0:T(128)} %moving.5) | copy-start | bytes 388
  3.8 7.6 %copy-start.4 = (s32[32]{0:T(128)S(1)}, s32[32]{0:T(128)}, u32[]{:S(2)}) copy-start(s32[32]{0:T(128)} %destination.3) | copy-start | bytes 388
  3.8 37.5 %all-to-all-start = ((bf16[32,256,128]{2,1,0:T(8,128)(2,1)}), bf16[32,256,128]{2,1,0:T(8,128)(2,1)S(1)}, u32[]{:S(2)}, u32[]{:S(2)}) async-start(bf16[32,256,128]{2,1,0:T(8,128)(2,1)} %bitcast.17), calls=%async_computation | async-start | bytes 4194304 | tf_op jit(solution)/shard_map/all_to_all | solution.py:270
  16.4 9.4 %collective-permute-start.3 = (bf16[64,512]{1,0:T(8,128)(2,1)S(1)}, bf16[64,512]{1,0:T(8,128)(2,1)S(1)}, u32[]{:S(2)}, u32[]{:S(2)}) collective-permute-start(bf16[64,512]{1,0:T(8,128)(2,1)S(1)} %get-tuple-element.36), channel_id=1, source_target_pairs={{0,2},{1,3},{2,4},{3,5},{4,6},{5,7},{6,0},{7,1},{8,10},{9,11},{10,... | collective-permute-start | bytes 196616 | tf_op jit(solution)/shard_map/ppermute | solution.py:234
  20.9 8.6 %collective-permute-start.5 = (bf16[64,512]{1,0:T(8,128)(2,1)S(1)}, bf16[64,512]{1,0:T(8,128)(2,1)S(1)}, u32[]{:S(2)}, u32[]{:S(2)}) collective-permute-start(bf16[64,512]{1,0:T(8,128)(2,1)S(1)} %get-tuple-element.39), channel_id=1, source_target_pairs={{0,6},{1,7},{2,0},{3,1},{4,2},{5,3},{6,4},{7,5},{8,14},{9,15},{10,... | collective-permute-start | bytes 196616 | tf_op jit(solution)/shard_map/ppermute | solution.py:234
  20.9 12.6 %collective-permute-start = (bf16[128,512]{1,0:T(8,128)(2,1)S(1)}, bf16[128,512]{1,0:T(8,128)(2,1)S(1)}, u32[]{:S(2)}, u32[]{:S(2)}) collective-permute-start(bf16[128,512]{1,0:T(8,128)(2,1)S(1)} %get-tuple-element.32), channel_id=1, source_target_pairs={{0,1},{1,2},{2,3},{3,4},{4,5},{5,6},{6,7},{7,0},{8,9},{9,10},{10,1... | collective-permute-start | bytes 393224 | tf_op jit(solution)/shard_map/ppermute | solution.py:234
  22.0 11.5 %collective-permute-start.1 = (bf16[128,512]{1,0:T(8,128)(2,1)S(1)}, bf16[128,512]{1,0:T(8,128)(2,1)S(1)}, u32[]{:S(2)}, u32[]{:S(2)}) collective-permute-start(bf16[128,512]{1,0:T(8,128)(2,1)S(1)} %get-tuple-element.33), channel_id=1, source_target_pairs={{0,7},{1,0},{2,1},{3,2},{4,3},{5,4},{6,5},{7,6},{8,15},{9,8},{10,9... | collective-permute-start | bytes 393224 | tf_op jit(solution)/shard_map/ppermute | solution.py:234
  23.0 6.6 %collective-permute-start.2 = (bf16[128,512]{1,0:T(8,128)(2,1)S(1)}, bf16[128,512]{1,0:T(8,128)(2,1)S(1)}, u32[]{:S(2)}, u32[]{:S(2)}) collective-permute-start(bf16[128,512]{1,0:T(8,128)(2,1)S(1)} %get-tuple-element.35), channel_id=1, source_target_pairs={{0,1},{1,2},{2,3},{3,4},{4,5},{5,6},{6,7},{7,0},{8,9},{9,10},{10,1... | collective-permute-start | bytes 393224 | tf_op jit(solution)/shard_map/ppermute | solution.py:234
  25.8 7.7 %collective-permute-start.4 = (bf16[128,512]{1,0:T(8,128)(2,1)S(1)}, bf16[128,512]{1,0:T(8,128)(2,1)S(1)}, u32[]{:S(2)}, u32[]{:S(2)}) collective-permute-start(bf16[128,512]{1,0:T(8,128)(2,1)S(1)} %get-tuple-element.38), channel_id=1, source_target_pairs={{0,7},{1,0},{2,1},{3,2},{4,3},{5,4},{6,5},{7,6},{8,15},{9,8},{10,9... | collective-permute-start | bytes 393224 | tf_op jit(solution)/shard_map/ppermute | solution.py:234
  43.5 34.1 %all-to-all-start.1 = ((bf16[32,256,128]{2,1,0:T(8,128)(2,1)}), bf16[32,256,128]{2,1,0:T(8,128)(2,1)S(1)}, u32[]{:S(2)}, u32[]{:S(2)}) async-start(bf16[32,256,128]{2,1,0:T(8,128)(2,1)} %gather_fusion), calls=%async_computation.1 | async-start | bytes 4194304 | tf_op jit(solution)/shard_map/all_to_all | solution.py:275
  47.5 10.4 %collective-permute-start.6 = (bf16[128,512]{1,0:T(8,128)(2,1)S(1)}, bf16[128,512]{1,0:T(8,128)(2,1)S(1)}, u32[]{:S(2)}, u32[]{:S(2)}) collective-permute-start(bf16[128,512]{1,0:T(8,128)(2,1)S(1)} %add_convert_fusion.5), channel_id=1, source_target_pairs={{0,2},{1,3},{2,4},{3,5},{4,6},{5,7},{6,0},{7,1},{8,10},{9,11},{10,... | collective-permute-start | bytes 393224 | tf_op jit(solution)/shard_map/ppermute | solution.py:234
  52.1 10.1 %collective-permute-start.7 = (bf16[128,512]{1,0:T(8,128)(2,1)S(1)}, bf16[128,512]{1,0:T(8,128)(2,1)S(1)}, u32[]{:S(2)}, u32[]{:S(2)}) collective-permute-start(bf16[128,512]{1,0:T(8,128)(2,1)S(1)} %add_convert_fusion.4), channel_id=1, source_target_pairs={{0,6},{1,7},{2,0},{3,1},{4,2},{5,3},{6,4},{7,5},{8,14},{9,15},{10,... | collective-permute-start | bytes 393224 | tf_op jit(solution)/shard_map/ppermute | solution.py:234
  83.5 11.2 %collective-permute-start.10 = (bf16[128,512]{1,0:T(8,128)(2,1)S(1)}, bf16[128,512]{1,0:T(8,128)(2,1)S(1)}, u32[]{:S(2)}, u32[]{:S(2)}) collective-permute-start(bf16[128,512]{1,0:T(8,128)(2,1)S(1)} %get-tuple-element.53), channel_id=1, source_target_pairs={{0,1},{1,2},{2,3},{3,4},{4,5},{5,6},{6,7},{7,0},{8,9},{9,10},{10,1... | collective-permute-start | bytes 393224 | tf_op jit(solution)/shard_map/ppermute | solution.py:234
  85.5 6.7 %collective-permute-start.11 = (bf16[64,512]{1,0:T(8,128)(2,1)S(1)}, bf16[64,512]{1,0:T(8,128)(2,1)S(1)}, u32[]{:S(2)}, u32[]{:S(2)}) collective-permute-start(bf16[64,512]{1,0:T(8,128)(2,1)S(1)} %get-tuple-element.54), channel_id=1, source_target_pairs={{0,2},{1,3},{2,4},{3,5},{4,6},{5,7},{6,0},{7,1},{8,10},{9,11},{10,... | collective-permute-start | bytes 196616 | tf_op jit(solution)/shard_map/ppermute | solution.py:234
  89.1 8.0 %collective-permute-start.14 = (bf16[64,512]{1,0:T(8,128)(2,1)S(1)}, bf16[64,512]{1,0:T(8,128)(2,1)S(1)}, u32[]{:S(2)}, u32[]{:S(2)}) collective-permute-start(bf16[64,512]{1,0:T(8,128)(2,1)S(1)} %get-tuple-element.57), channel_id=1, source_target_pairs={{0,6},{1,7},{2,0},{3,1},{4,2},{5,3},{6,4},{7,5},{8,14},{9,15},{10,... | collective-permute-start | bytes 196616 | tf_op jit(solution)/shard_map/ppermute | solution.py:234
  89.1 12.5 %collective-permute-start.8 = (bf16[128,512]{1,0:T(8,128)(2,1)S(1)}, bf16[128,512]{1,0:T(8,128)(2,1)S(1)}, u32[]{:S(2)}, u32[]{:S(2)}) collective-permute-start(bf16[128,512]{1,0:T(8,128)(2,1)S(1)} %get-tuple-element.50), channel_id=1, source_target_pairs={{0,1},{1,2},{2,3},{3,4},{4,5},{5,6},{6,7},{7,0},{8,9},{9,10},{10,1... | collective-permute-start | bytes 393224 | tf_op jit(solution)/shard_map/ppermute | solution.py:234
  91.5 10.0 %collective-permute-start.9 = (bf16[128,512]{1,0:T(8,128)(2,1)S(1)}, bf16[128,512]{1,0:T(8,128)(2,1)S(1)}, u32[]{:S(2)}, u32[]{:S(2)}) collective-permute-start(bf16[128,512]{1,0:T(8,128)(2,1)S(1)} %get-tuple-element.51), channel_id=1, source_target_pairs={{0,7},{1,0},{2,1},{3,2},{4,3},{5,4},{6,5},{7,6},{8,15},{9,8},{10,9... | collective-permute-start | bytes 393224 | tf_op jit(solution)/shard_map/ppermute | solution.py:234
  92.2 7.1 %collective-permute-start.13 = (bf16[128,512]{1,0:T(8,128)(2,1)S(1)}, bf16[128,512]{1,0:T(8,128)(2,1)S(1)}, u32[]{:S(2)}, u32[]{:S(2)}) collective-permute-start(bf16[128,512]{1,0:T(8,128)(2,1)S(1)} %get-tuple-element.56), channel_id=1, source_target_pairs={{0,7},{1,0},{2,1},{3,2},{4,3},{5,4},{6,5},{7,6},{8,15},{9,8},{10,9... | collective-permute-start | bytes 393224 | tf_op jit(solution)/shard_map/ppermute | solution.py:234
  94.7 6.8 %collective-permute-start.12 = (bf16[128,512]{1,0:T(8,128)(2,1)S(1)}, bf16[128,512]{1,0:T(8,128)(2,1)S(1)}, u32[]{:S(2)}, u32[]{:S(2)}) collective-permute-start(bf16[128,512]{1,0:T(8,128)(2,1)S(1)} %add_convert_fusion.2), channel_id=1, source_target_pairs={{0,2},{1,3},{2,4},{3,5},{4,6},{5,7},{6,0},{7,1},{8,10},{9,11},{10,... | collective-permute-start | bytes 393224 | tf_op jit(solution)/shard_map/ppermute | solution.py:234
  99.3 8.8 %collective-permute-start.15 = (bf16[128,512]{1,0:T(8,128)(2,1)S(1)}, bf16[128,512]{1,0:T(8,128)(2,1)S(1)}, u32[]{:S(2)}, u32[]{:S(2)}) collective-permute-start(bf16[128,512]{1,0:T(8,128)(2,1)S(1)} %add_convert_fusion.1), channel_id=1, source_target_pairs={{0,6},{1,7},{2,0},{3,1},{4,2},{5,3},{6,4},{7,5},{8,14},{9,15},{10,... | collective-permute-start | bytes 393224 | tf_op jit(solution)/shard_map/ppermute | solution.py:234
where the time goes:
time: 109 us
  waiting for transfers between devices  49 us (45%)
  starting transfers between devices  40.3 us (37%)
  Pallas kernels  13.9 us (13%)
  local copies, waits for them, and re-layouts  2.93 us (3%)
  other arithmetic  1.93 us (2%)
    ppermute x16, starting transfers between devices, shift(): lax.ppermute(block, 'tp', [(i, (i + k) % peers) for i in range(peers)])  28.9 us
    ppermute x16, waiting for transfers between devices, shift(): lax.ppermute(block, 'tp', [(i, (i + k) % peers) for i in range(peers)])  25.9 us
    all_to_all x1, waiting for transfers between devices, on_device(): arrived = lax.all_to_all(ordered, REP, 0, 0, tiled=True)  15.3 us
    pallas_call x2, Pallas kernels, run_slot(): pl.pallas_call(functools.partial(slot_kernel, held is not None, group, CH...  10.8 us
    all_to_all x1, waiting for transfers between devices, on_device(): spread = lax.all_to_all(sent, REP, 0, 0, tiled=True)  7.84 us
    all_to_all x1, starting transfers between devices, on_device(): spread = lax.all_to_all(sent, REP, 0, 0, tiled=True)  7.46 us
    all_to_all x1, starting transfers between devices, on_device(): arrived = lax.all_to_all(ordered, REP, 0, 0, tiled=True)  4.01 us
    pallas_call x1, Pallas kernels, pick(): pl.pallas_call(pick_kernel, out_shape=jax.ShapeDtypeStruct((2 * rows, HEA...  3.11 us
  transfers between devices with their start and end apart: 18, of which 9 were waited for; matrix products, arithmetic and copies ran while one was open for 2% of the time, Pallas kernels for 5%

commit v1 on v0

--- a/solution.py
+++ b/solution.py
@@ -136,12 +136,13 @@
             for copy in save(c):
                 copy.start()
 
-        @pl.when(c * chunk < length)
-        def _():
+        def absorb(partly):
             piece = pl.ds(pl.multiple_of(c * chunk, chunk), chunk)
             scores = lax.dot_general(kept(0, piece)[...], grouped, over_head, preferred_element_type=jnp.float32)
-            seen = lax.broadcasted_iota(jnp.int32, (chunk, rows), 0) < length - c * chunk
-            scores = jnp.where(seen, scores * factor, MASKED)
+            scores = scores * factor
+            if partly:
+                seen = lax.broadcasted_iota(jnp.int32, (chunk, rows), 0) < length - c * chunk
+                scores = jnp.where(seen, scores, MASKED)
             before = top_ref[...]
             top = jnp.maximum(before, jnp.max(scores, axis=0, keepdims=True))
             shrink = jnp.exp2(before - top)
@@ -152,6 +153,9 @@
                 kept(1, piece)[...], weights.astype(jnp.bfloat16), over_keys, preferred_element_type=jnp.float32
             )
 
+        whole = (c + 1) * chunk <= length
+        pl.when(whole)(functools.partial(absorb, False))
+        pl.when(jnp.logical_and(c * chunk < length, jnp.logical_not(whole)))(functools.partial(absorb, True))
         return 0
 
     lax.fori_loop(0, chunks, step, 0)
@@ -162,7 +166,8 @@
     width = wbuf.shape[1] // peers
     out = 0
     for k in range(peers):
-        columns = pl.ds(pl.multiple_of(lax.rem(me + k, peers) * width, width), width)
+        owner = lax.rem(me + jnp.where(lax.rem(own, 2) == 0, k, peers - k), peers)
+        columns = pl.ds(pl.multiple_of(owner * width, width), width)
         block = jnp.dot(obuf[...], wbuf[:, columns], preferred_element_type=jnp.float32)
         block = block.astype(jnp.bfloat16)
         height = span // parts[k]
@@ -231,7 +236,9 @@
 
 def shift(block, k):
     peers = lax.axis_size("tp")
-    return lax.ppermute(block, "tp", [(i, (i + k) % peers) for i in range(peers)])
+    pairs = [(i, (i + k) % peers) for i in range(peers)]
+    pairs += [(peers + i, peers + (i - k) % peers) for i in range(peers)]
+    return lax.ppermute(block, ("rep_2", "tp"), pairs)
 
 
 def widen(block):

time: 109 us -> 110 us (level); the launches traced: 109 us -> 108 us
    ppermute x16, waiting for transfers between devices: 25.9 us -> 22.3 us  [shift(): return lax.ppermute(block, ('rep_2', 'tp'), pairs)]
    all_to_all x1, waiting for transfers between devices: 15.3 us -> 17.2 us  [on_device(): arrived = lax.all_to_all(ordered, REP, 0, 0, tiled=True)]
    all_to_all x1, waiting for transfers between devices: 7.84 us -> 9.24 us  [on_device(): spread = lax.all_to_all(sent, REP, 0, 0, tiled=True)]
  transfers between devices with their start and end apart: 18 -> 18, of which waited for: 9 -> 10; matrix products, arithmetic and copies ran while one was open for 2% -> 2% of each run, Pallas kernels for 5% -> 5%
where the time goes in v1:
time: 110 us; the launch traced here: 108 us
  waiting for transfers between devices  48.8 us (44%)
  starting transfers between devices  39.9 us (36%)
  Pallas kernels  13.9 us (13%)
  local copies, waits for them, and re-layouts  2.93 us (3%)
  other arithmetic  1.93 us (2%)
    ppermute x16, starting transfers between devices, shift(): return lax.ppermute(block, ('rep_2', 'tp'), pairs)  28.4 us
    ppermute x16, waiting for transfers between devices, shift(): return lax.ppermute(block, ('rep_2', 'tp'), pairs)  22.3 us
    all_to_all x1, waiting for transfers between devices, on_device(): arrived = lax.all_to_all(ordered, REP, 0, 0, tiled=True)  17.2 us
    pallas_call x2, Pallas kernels, run_slot(): pl.pallas_call(functools.partial(slot_kernel, held is not None, group, CH...  10.8 us
    all_to_all x1, waiting for transfers between devices, on_device(): spread = lax.all_to_all(sent, REP, 0, 0, tiled=True)  9.24 us
    all_to_all x1, starting transfers between devices, on_device(): spread = lax.all_to_all(sent, REP, 0, 0, tiled=True)  7.46 us
    all_to_all x1, starting transfers between devices, on_device(): arrived = lax.all_to_all(ordered, REP, 0, 0, tiled=True)  4.01 us
    pallas_call x1, Pallas kernels, pick(): pl.pallas_call(pick_kernel, out_shape=jax.ShapeDtypeStruct((2 * rows, HEA...  3.11 us
  transfers between devices with their start and end apart: 18, of which 10 were waited for; matrix products, arithmetic and copies ran while one was open for 2% of the time, Pallas kernels for 5%

profile of v1, /device:TPU:64, one launch (start us, length us, event | category | flops | bytes accessed | tf_op | source)
XLA Modules:
  0.0 108.3 jit_solution(15513573825546998562)
XLA Ops:
  0.6 3.1 %pick.1 = bf16[8192,128]{1,0:T(8,128)(2,1)} custom-call(s32[32]{0:T(128)} %moving.5, bf16[2,8192,128]{2,1,0:T(8,128)(2,1)} %bitcast.16), custom_call_target="tpu_custom_call" | custom-call | bytes 4194304 | tf_op jit(solution)/shard_map/pick/pallas_call | solution.py:50
  3.8 7.5 %all-to-all-start = ((bf16[32,256,128]{2,1,0:T(8,128)(2,1)}), bf16[32,256,128]{2,1,0:T(8,128)(2,1)S(1)}, u32[]{:S(2)}, u32[]{:S(2)}) async-start(bf16[32,256,128]{2,1,0:T(8,128)(2,1)} %bitcast.17), calls=%async_computation | async-start | bytes 4194304 | tf_op jit(solution)/shard_map/all_to_all | solution.py:277
  11.3 0.1 copy.13.lengths
  11.4 5.0 %slot.2 = (bf16[2,2,4096,128]{3,2,1,0:T(8,128)(2,1)}, bf16[128,512]{1,0:T(8,128)(2,1)S(1)}, bf16[128,512]{1,0:T(8,128)(2,1)S(1)}, bf16[128,512]{1,0:T(8,128)(2,1...) custom-call(s32[32,2]{1,0:T(8,128)S(1)} %copy.13.lengths, ...), custom_call_target="tpu_custom_call" | custom-call | flops 1644167168 | bytes 8388608 | tf_op jit(solution)/shard_map/slot/pallas_call | solution.py:209
  16.4 4.5 %collective-permute-start.3 = (bf16[64,512]{1,0:T(8,128)(2,1)S(1)}, bf16[64,512]{1,0:T(8,128)(2,1)S(1)}, u32[]{:S(2)}, u32[]{:S(2)}) collective-permute-start(bf16[64,512]{1,0:T(8,128)(2,1)S(1)} %get-tuple-element.36), channel_id=1, source_target_pairs={{0,2},{1,3},{2,4},{3,5},{4,6},{5,7},{6,0},{7,1},{8,14},{9,15},{10,... | collective-permute-start | bytes 196616 | tf_op jit(solution)/shard_map/ppermute | solution.py:241
  20.9 1.0 collective-permute-start
  22.0 1.0 collective-permute-start.1
  23.0 2.7 %collective-permute-start.2 = (bf16[128,512]{1,0:T(8,128)(2,1)S(1)}, bf16[128,512]{1,0:T(8,128)(2,1)S(1)}, u32[]{:S(2)}, u32[]{:S(2)}) collective-permute-start(bf16[128,512]{1,0:T(8,128)(2,1)S(1)} %get-tuple-element.35), channel_id=1, source_target_pairs={{0,1},{1,2},{2,3},{3,4},{4,5},{5,6},{6,7},{7,0},{8,15},{9,8},{10,9... | collective-permute-start | bytes 393224 | tf_op jit(solution)/shard_map/ppermute | solution.py:241
  25.6 0.1 select_reduce_fusion
  25.9 4.9 %collective-permute-done.2 = bf16[128,512]{1,0:T(8,128)(2,1)S(1)} collective-permute-done((bf16[128,512]{1,0:T(8,128)(2,1)S(1)}, bf16[128,512]{1,0:T(8,128)(2,1)S(1)}, u32[]{:S(2)}, u32[]{:S(2)}) %collective-permute-start.2) | collective-permute-done | bytes 131104 | tf_op jit(solution)/shard_map/ppermute | solution.py:241
  30.8 1.2 %collective-permute-done.4 = bf16[128,512]{1,0:T(8,128)(2,1)S(1)} collective-permute-done((bf16[128,512]{1,0:T(8,128)(2,1)S(1)}, bf16[128,512]{1,0:T(8,128)(2,1)S(1)}, u32[]{:S(2)}, u32[]{:S(2)}) %collective-permute-start.4) | collective-permute-done | bytes 131104 | tf_op jit(solution)/shard_map/ppermute | solution.py:241
  32.1 9.2 %all-to-all-done = bf16[32,256,128]{2,1,0:T(8,128)(2,1)S(1)} async-done(((bf16[32,256,128]{2,1,0:T(8,128)(2,1)}), bf16[32,256,128]{2,1,0:T(8,128)(2,1)S(1)}, u32[]{:S(2)}, u32[]{:S(2)}) %all-to-all-start) | async-done | bytes 2097184 | tf_op jit(solution)/shard_map/all_to_all | solution.py:277
  41.4 2.1 %gather_fusion = bf16[32,256,128]{2,1,0:T(8,128)(2,1)} fusion(bf16[32,256,128]{2,1,0:T(8,128)(2,1)S(1)} %all-to-all-done, s32[1024]{0:T(1024)S(1)} %pad_clamp_fusion), kind=kCustom, calls=%fused_computation | custom fusion | bytes 4194432 | tf_op jit(solution)/shard_map/gather | solution.py:281
  43.5 4.0 %all-to-all-start.1 = ((bf16[32,256,128]{2,1,0:T(8,128)(2,1)}), bf16[32,256,128]{2,1,0:T(8,128)(2,1)S(1)}, u32[]{:S(2)}, u32[]{:S(2)}) async-start(bf16[32,256,128]{2,1,0:T(8,128)(2,1)} %gather_fusion), calls=%async_computation.1 | async-start | bytes 4194304 | tf_op jit(solution)/shard_map/all_to_all | solution.py:282
  47.5 4.6 %collective-permute-start.6 = (bf16[128,512]{1,0:T(8,128)(2,1)S(1)}, bf16[128,512]{1,0:T(8,128)(2,1)S(1)}, u32[]{:S(2)}, u32[]{:S(2)}) collective-permute-start(bf16[128,512]{1,0:T(8,128)(2,1)S(1)} %add_convert_fusion.5), channel_id=1, source_target_pairs={{0,2},{1,3},{2,4},{3,5},{4,6},{5,7},{6,0},{7,1},{8,14},{9,15},{10,... | collective-permute-start | bytes 393224 | tf_op jit(solution)/shard_map/ppermute | solution.py:241
  52.1 0.6 dynamic_slice.3
  52.7 0.7 iota_compare_fusion.1
  53.3 4.8 %collective-permute-done.6 = bf16[128,512]{1,0:T(8,128)(2,1)S(1)} collective-permute-done((bf16[128,512]{1,0:T(8,128)(2,1)S(1)}, bf16[128,512]{1,0:T(8,128)(2,1)S(1)}, u32[]{:S(2)}, u32[]{:S(2)}) %collective-permute-start.6) | collective-permute-done | bytes 131104 | tf_op jit(solution)/shard_map/ppermute | solution.py:241
  58.1 2.2 %collective-permute-done.7 = bf16[128,512]{1,0:T(8,128)(2,1)S(1)} collective-permute-done((bf16[128,512]{1,0:T(8,128)(2,1)S(1)}, bf16[128,512]{1,0:T(8,128)(2,1)S(1)}, u32[]{:S(2)}, u32[]{:S(2)}) %collective-permute-start.7) | collective-permute-done | bytes 131104 | tf_op jit(solution)/shard_map/ppermute | solution.py:241
  60.4 17.2 %all-to-all-done.1 = bf16[32,256,128]{2,1,0:T(8,128)(2,1)S(1)} async-done(((bf16[32,256,128]{2,1,0:T(8,128)(2,1)}), bf16[32,256,128]{2,1,0:T(8,128)(2,1)S(1)}, u32[]{:S(2)}, u32[]{:S(2)}) %all-to-all-start.1) | async-done | bytes 2097184 | tf_op jit(solution)/shard_map/all_to_all | solution.py:282
  77.6 5.9 %slot.3 = (bf16[2,2,4096,128]{3,2,1,0:T(8,128)(2,1)}, bf16[128,512]{1,0:T(8,128)(2,1)S(1)}, bf16[128,512]{1,0:T(8,128)(2,1)S(1)}, bf16[128,512]{1,0:T(8,128)(2,1...) custom-call(s32[32,2]{1,0:T(8,128)S(1)} %copy.13.lengths, ...), custom_call_target="tpu_custom_call", output_to_operand_aliasing={{0}: (8, {})} | custom-call | flops 1644167168 | bytes 8388608 | tf_op jit(solution)/shard_map/slot/pallas_call | solution.py:209
  83.5 2.0 %collective-permute-start.10 = (bf16[128,512]{1,0:T(8,128)(2,1)S(1)}, bf16[128,512]{1,0:T(8,128)(2,1)S(1)}, u32[]{:S(2)}, u32[]{:S(2)}) collective-permute-start(bf16[128,512]{1,0:T(8,128)(2,1)S(1)} %get-tuple-element.53), channel_id=1, source_target_pairs={{0,1},{1,2},{2,3},{3,4},{4,5},{5,6},{6,7},{7,0},{8,15},{9,8},{10,9... | collective-permute-start | bytes 393224 | tf_op jit(solution)/shard_map/ppermute | solution.py:241
  85.5 3.6 %collective-permute-start.11 = (bf16[64,512]{1,0:T(8,128)(2,1)S(1)}, bf16[64,512]{1,0:T(8,128)(2,1)S(1)}, u32[]{:S(2)}, u32[]{:S(2)}) collective-permute-start(bf16[64,512]{1,0:T(8,128)(2,1)S(1)} %get-tuple-element.54), channel_id=1, source_target_pairs={{0,2},{1,3},{2,4},{3,5},{4,6},{5,7},{6,0},{7,1},{8,14},{9,15},{10,... | collective-permute-start | bytes 196616 | tf_op jit(solution)/shard_map/ppermute | solution.py:241
  89.1 2.5 %collective-permute-start.8 = (bf16[128,512]{1,0:T(8,128)(2,1)S(1)}, bf16[128,512]{1,0:T(8,128)(2,1)S(1)}, u32[]{:S(2)}, u32[]{:S(2)}) collective-permute-start(bf16[128,512]{1,0:T(8,128)(2,1)S(1)} %get-tuple-element.50), channel_id=1, source_target_pairs={{0,1},{1,2},{2,3},{3,4},{4,5},{5,6},{6,7},{7,0},{8,15},{9,8},{10,9... | collective-permute-start | bytes 393224 | tf_op jit(solution)/shard_map/ppermute | solution.py:241
  91.5 0.7 collective-permute-done.11
  92.2 0.6 collective-permute-start.13
  92.9 4.4 %collective-permute-start.12 = (bf16[128,512]{1,0:T(8,128)(2,1)S(1)}, bf16[128,512]{1,0:T(8,128)(2,1)S(1)}, u32[]{:S(2)}, u32[]{:S(2)}) collective-permute-start(bf16[128,512]{1,0:T(8,128)(2,1)S(1)} %add_convert_fusion.2), channel_id=1, source_target_pairs={{0,2},{1,3},{2,4},{3,5},{4,6},{5,7},{6,0},{7,1},{8,14},{9,15},{10,... | collective-permute-start | bytes 393224 | tf_op jit(solution)/shard_map/ppermute | solution.py:241
  97.3 2.9 %collective-permute-done.13 = bf16[128,512]{1,0:T(8,128)(2,1)S(1)} collective-permute-done((bf16[128,512]{1,0:T(8,128)(2,1)S(1)}, bf16[128,512]{1,0:T(8,128)(2,1)S(1)}, u32[]{:S(2)}, u32[]{:S(2)}) %collective-permute-start.13) | collective-permute-done | bytes 131104 | tf_op jit(solution)/shard_map/ppermute | solution.py:241
  100.2 1.4 %collective-permute-start.15 = (bf16[128,512]{1,0:T(8,128)(2,1)S(1)}, bf16[128,512]{1,0:T(8,128)(2,1)S(1)}, u32[]{:S(2)}, u32[]{:S(2)}) collective-permute-start(bf16[128,512]{1,0:T(8,128)(2,1)S(1)} %add_convert_fusion.1), channel_id=1, source_target_pairs={{0,6},{1,7},{2,0},{3,1},{4,2},{5,3},{6,4},{7,5},{8,10},{9,11},{10,... | collective-permute-start | bytes 393224 | tf_op jit(solution)/shard_map/ppermute | solution.py:241
  101.7 0.3 collective-permute-done.12
  102.0 5.4 %collective-permute-done.15 = bf16[128,512]{1,0:T(8,128)(2,1)S(1)} collective-permute-done((bf16[128,512]{1,0:T(8,128)(2,1)S(1)}, bf16[128,512]{1,0:T(8,128)(2,1)S(1)}, u32[]{:S(2)}, u32[]{:S(2)}) %collective-permute-start.15) | collective-permute-done | bytes 131104 | tf_op jit(solution)/shard_map/ppermute | solution.py:241
  107.4 0.8 bitcast_select_fusion
  (34 shorter events, 0.6 us)
Async XLA Ops:
  3.7 7.5 %copy-start.5 = (s32[32,2]{0,1:T(2,128)S(1)}, s32[32,2]{0,1:T(2,128)}, u32[]{:S(2)}) copy-start(s32[32,2]{0,1:T(2,128)} %param.12) | copy-start | bytes 772
  3.8 7.6 %copy-start = (bf16[256,512]{1,0:T(8,128)(2,1)S(1)}, bf16[256,512]{1,0:T(8,128)(2,1)}, u32[]{:S(2)}) copy-start(bf16[256,512]{1,0:T(8,128)(2,1)} %queries.3) | copy-start | bytes 786436
  3.8 7.6 %copy-start.1 = (bf16[256,128]{1,0:T(8,128)(2,1)S(1)}, bf16[256,128]{1,0:T(8,128)(2,1)}, u32[]{:S(2)}) copy-start(bf16[256,128]{1,0:T(8,128)(2,1)} %keys_new.3) | copy-start | bytes 196612
  3.8 7.6 %copy-start.2 = (bf16[256,128]{1,0:T(8,128)(2,1)S(1)}, bf16[256,128]{1,0:T(8,128)(2,1)}, u32[]{:S(2)}) copy-start(bf16[256,128]{1,0:T(8,128)(2,1)} %values_new.3) | copy-start | bytes 196612
  3.8 7.6 %copy-start.3 = (s32[32]{0:T(128)S(1)}, s32[32]{0:T(128)}, u32[]{:S(2)}) copy-start(s32[32]{0:T(128)} %moving.5) | copy-start | bytes 388
  3.8 7.6 %copy-start.4 = (s32[32]{0:T(128)S(1)}, s32[32]{0:T(128)}, u32[]{:S(2)}) copy-start(s32[32]{0:T(128)} %destination.3) | copy-start | bytes 388
  3.8 37.5 %all-to-all-start = ((bf16[32,256,128]{2,1,0:T(8,128)(2,1)}), bf16[32,256,128]{2,1,0:T(8,128)(2,1)S(1)}, u32[]{:S(2)}, u32[]{:S(2)}) async-start(bf16[32,256,128]{2,1,0:T(8,128)(2,1)} %bitcast.17), calls=%async_computation | async-start | bytes 4194304 | tf_op jit(solution)/shard_map/all_to_all | solution.py:277
  16.4 9.4 %collective-permute-start.3 = (bf16[64,512]{1,0:T(8,128)(2,1)S(1)}, bf16[64,512]{1,0:T(8,128)(2,1)S(1)}, u32[]{:S(2)}, u32[]{:S(2)}) collective-permute-start(bf16[64,512]{1,0:T(8,128)(2,1)S(1)} %get-tuple-element.36), channel_id=1, source_target_pairs={{0,2},{1,3},{2,4},{3,5},{4,6},{5,7},{6,0},{7,1},{8,14},{9,15},{10,... | collective-permute-start | bytes 196616 | tf_op jit(solution)/shard_map/ppermute | solution.py:241
  20.9 9.9 %collective-permute-start.5 = (bf16[64,512]{1,0:T(8,128)(2,1)S(1)}, bf16[64,512]{1,0:T(8,128)(2,1)S(1)}, u32[]{:S(2)}, u32[]{:S(2)}) collective-permute-start(bf16[64,512]{1,0:T(8,128)(2,1)S(1)} %get-tuple-element.39), channel_id=1, source_target_pairs={{0,6},{1,7},{2,0},{3,1},{4,2},{5,3},{6,4},{7,5},{8,10},{9,11},{10,... | collective-permute-start | bytes 196616 | tf_op jit(solution)/shard_map/ppermute | solution.py:241
  20.9 11.2 %collective-permute-start = (bf16[128,512]{1,0:T(8,128)(2,1)S(1)}, bf16[128,512]{1,0:T(8,128)(2,1)S(1)}, u32[]{:S(2)}, u32[]{:S(2)}) collective-permute-start(bf16[128,512]{1,0:T(8,128)(2,1)S(1)} %get-tuple-element.32), channel_id=1, source_target_pairs={{0,1},{1,2},{2,3},{3,4},{4,5},{5,6},{6,7},{7,0},{8,15},{9,8},{10,9... | collective-permute-start | bytes 393224 | tf_op jit(solution)/shard_map/ppermute | solution.py:241
  22.0 10.1 %collective-permute-start.1 = (bf16[128,512]{1,0:T(8,128)(2,1)S(1)}, bf16[128,512]{1,0:T(8,128)(2,1)S(1)}, u32[]{:S(2)}, u32[]{:S(2)}) collective-permute-start(bf16[128,512]{1,0:T(8,128)(2,1)S(1)} %get-tuple-element.33), channel_id=1, source_target_pairs={{0,7},{1,0},{2,1},{3,2},{4,3},{5,4},{6,5},{7,6},{8,9},{9,10},{10,1... | collective-permute-start | bytes 393224 | tf_op jit(solution)/shard_map/ppermute | solution.py:241
  23.0 7.8 %collective-permute-start.2 = (bf16[128,512]{1,0:T(8,128)(2,1)S(1)}, bf16[128,512]{1,0:T(8,128)(2,1)S(1)}, u32[]{:S(2)}, u32[]{:S(2)}) collective-permute-start(bf16[128,512]{1,0:T(8,128)(2,1)S(1)} %get-tuple-element.35), channel_id=1, source_target_pairs={{0,1},{1,2},{2,3},{3,4},{4,5},{5,6},{6,7},{7,0},{8,15},{9,8},{10,9... | collective-permute-start | bytes 393224 | tf_op jit(solution)/shard_map/ppermute | solution.py:241
  25.8 6.3 %collective-permute-start.4 = (bf16[128,512]{1,0:T(8,128)(2,1)S(1)}, bf16[128,512]{1,0:T(8,128)(2,1)S(1)}, u32[]{:S(2)}, u32[]{:S(2)}) collective-permute-start(bf16[128,512]{1,0:T(8,128)(2,1)S(1)} %get-tuple-element.38), channel_id=1, source_target_pairs={{0,7},{1,0},{2,1},{3,2},{4,3},{5,4},{6,5},{7,6},{8,9},{9,10},{10,1... | collective-permute-start | bytes 393224 | tf_op jit(solution)/shard_map/ppermute | solution.py:241
  43.5 34.1 %all-to-all-start.1 = ((bf16[32,256,128]{2,1,0:T(8,128)(2,1)}), bf16[32,256,128]{2,1,0:T(8,128)(2,1)S(1)}, u32[]{:S(2)}, u32[]{:S(2)}) async-start(bf16[32,256,128]{2,1,0:T(8,128)(2,1)} %gather_fusion), calls=%async_computation.1 | async-start | bytes 4194304 | tf_op jit(solution)/shard_map/all_to_all | solution.py:282
  47.5 10.6 %collective-permute-start.6 = (bf16[128,512]{1,0:T(8,128)(2,1)S(1)}, bf16[128,512]{1,0:T(8,128)(2,1)S(1)}, u32[]{:S(2)}, u32[]{:S(2)}) collective-permute-start(bf16[128,512]{1,0:T(8,128)(2,1)S(1)} %add_convert_fusion.5), channel_id=1, source_target_pairs={{0,2},{1,3},{2,4},{3,5},{4,6},{5,7},{6,0},{7,1},{8,14},{9,15},{10,... | collective-permute-start | bytes 393224 | tf_op jit(solution)/shard_map/ppermute | solution.py:241
  52.1 8.2 %collective-permute-start.7 = (bf16[128,512]{1,0:T(8,128)(2,1)S(1)}, bf16[128,512]{1,0:T(8,128)(2,1)S(1)}, u32[]{:S(2)}, u32[]{:S(2)}) collective-permute-start(bf16[128,512]{1,0:T(8,128)(2,1)S(1)} %add_convert_fusion.4), channel_id=1, source_target_pairs={{0,6},{1,7},{2,0},{3,1},{4,2},{5,3},{6,4},{7,5},{8,10},{9,11},{10,... | collective-permute-start | bytes 393224 | tf_op jit(solution)/shard_map/ppermute | solution.py:241
  83.5 9.4 %collective-permute-start.10 = (bf16[128,512]{1,0:T(8,128)(2,1)S(1)}, bf16[128,512]{1,0:T(8,128)(2,1)S(1)}, u32[]{:S(2)}, u32[]{:S(2)}) collective-permute-start(bf16[128,512]{1,0:T(8,128)(2,1)S(1)} %get-tuple-element.53), channel_id=1, source_target_pairs={{0,1},{1,2},{2,3},{3,4},{4,5},{5,6},{6,7},{7,0},{8,15},{9,8},{10,9... | collective-permute-start | bytes 393224 | tf_op jit(solution)/shard_map/ppermute | solution.py:241
  85.5 6.7 %collective-permute-start.11 = (bf16[64,512]{1,0:T(8,128)(2,1)S(1)}, bf16[64,512]{1,0:T(8,128)(2,1)S(1)}, u32[]{:S(2)}, u32[]{:S(2)}) collective-permute-start(bf16[64,512]{1,0:T(8,128)(2,1)S(1)} %get-tuple-element.54), channel_id=1, source_target_pairs={{0,2},{1,3},{2,4},{3,5},{4,6},{5,7},{6,0},{7,1},{8,14},{9,15},{10,... | collective-permute-start | bytes 196616 | tf_op jit(solution)/shard_map/ppermute | solution.py:241
  89.1 8.2 %collective-permute-start.14 = (bf16[64,512]{1,0:T(8,128)(2,1)S(1)}, bf16[64,512]{1,0:T(8,128)(2,1)S(1)}, u32[]{:S(2)}, u32[]{:S(2)}) collective-permute-start(bf16[64,512]{1,0:T(8,128)(2,1)S(1)} %get-tuple-element.57), channel_id=1, source_target_pairs={{0,6},{1,7},{2,0},{3,1},{4,2},{5,3},{6,4},{7,5},{8,10},{9,11},{10,... | collective-permute-start | bytes 196616 | tf_op jit(solution)/shard_map/ppermute | solution.py:241
  89.1 12.6 %collective-permute-start.8 = (bf16[128,512]{1,0:T(8,128)(2,1)S(1)}, bf16[128,512]{1,0:T(8,128)(2,1)S(1)}, u32[]{:S(2)}, u32[]{:S(2)}) collective-permute-start(bf16[128,512]{1,0:T(8,128)(2,1)S(1)} %get-tuple-element.50), channel_id=1, source_target_pairs={{0,1},{1,2},{2,3},{3,4},{4,5},{5,6},{6,7},{7,0},{8,15},{9,8},{10,9... | collective-permute-start | bytes 393224 | tf_op jit(solution)/shard_map/ppermute | solution.py:241
  91.5 10.2 %collective-permute-start.9 = (bf16[128,512]{1,0:T(8,128)(2,1)S(1)}, bf16[128,512]{1,0:T(8,128)(2,1)S(1)}, u32[]{:S(2)}, u32[]{:S(2)}) collective-permute-start(bf16[128,512]{1,0:T(8,128)(2,1)S(1)} %get-tuple-element.51), channel_id=1, source_target_pairs={{0,7},{1,0},{2,1},{3,2},{4,3},{5,4},{6,5},{7,6},{8,9},{9,10},{10,1... | collective-permute-start | bytes 393224 | tf_op jit(solution)/shard_map/ppermute | solution.py:241
  92.2 7.9 %collective-permute-start.13 = (bf16[128,512]{1,0:T(8,128)(2,1)S(1)}, bf16[128,512]{1,0:T(8,128)(2,1)S(1)}, u32[]{:S(2)}, u32[]{:S(2)}) collective-permute-start(bf16[128,512]{1,0:T(8,128)(2,1)S(1)} %get-tuple-element.56), channel_id=1, source_target_pairs={{0,7},{1,0},{2,1},{3,2},{4,3},{5,4},{6,5},{7,6},{8,9},{9,10},{10,1... | collective-permute-start | bytes 393224 | tf_op jit(solution)/shard_map/ppermute | solution.py:241
  92.9 9.1 %collective-permute-start.12 = (bf16[128,512]{1,0:T(8,128)(2,1)S(1)}, bf16[128,512]{1,0:T(8,128)(2,1)S(1)}, u32[]{:S(2)}, u32[]{:S(2)}) collective-permute-start(bf16[128,512]{1,0:T(8,128)(2,1)S(1)} %add_convert_fusion.2), channel_id=1, source_target_pairs={{0,2},{1,3},{2,4},{3,5},{4,6},{5,7},{6,0},{7,1},{8,14},{9,15},{10,... | collective-permute-start | bytes 393224 | tf_op jit(solution)/shard_map/ppermute | solution.py:241
  100.2 7.2 %collective-permute-start.15 = (bf16[128,512]{1,0:T(8,128)(2,1)S(1)}, bf16[128,512]{1,0:T(8,128)(2,1)S(1)}, u32[]{:S(2)}, u32[]{:S(2)}) collective-permute-start(bf16[128,512]{1,0:T(8,128)(2,1)S(1)} %add_convert_fusion.1), channel_id=1, source_target_pairs={{0,6},{1,7},{2,0},{3,1},{4,2},{5,3},{6,4},{7,5},{8,10},{9,11},{10,... | collective-permute-start | bytes 393224 | tf_op jit(solution)/shard_map/ppermute | solution.py:241
